TPU v7x, 512 devices: a whole 4x8x8 slice. The times are simulated.
512 devices in a mesh: expert: 64 (over z, y), tensor: 8 (over x, core).
Axes of the slice: x: 4, y: 8, z: 8, core: 2. Of those that a mesh axis runs over, the one named last changes fastest.
Arguments:
- tokens: bfloat16 [3072, 4096], P('expert', 'tensor'), may hold values from -6 to 6
- cotangent: bfloat16 [3072, 4096], P('expert', 'tensor'), may hold values from -6 to 6
- expert_ids: int32 [3072, 8], P('expert'), may hold values from 0 to 63, all different within a row; in each aligned block of 48 rows (0 to 47, 48 to 95, ...) at most 8 rows name the same one
- gate_values: float32 [3072, 8], P('expert'), may hold values from 0.05 to 1
- w_gate: bfloat16 [64, 768, 4096], P('expert', 'tensor'), may hold values from -0.09375 to 0.09375
- w_up: bfloat16 [64, 768, 4096], P('expert', 'tensor'), may hold values from -0.09375 to 0.09375
- w_down: bfloat16 [64, 768, 4096], P('expert', 'tensor'), may hold values from -0.21875 to 0.21875
Outputs:
- grad_tokens: bfloat16 [3072, 4096], P('expert', 'tensor')
- grad_gate: bfloat16 [64, 768, 4096], P('expert', 'tensor')
- grad_up: bfloat16 [64, 768, 4096], P('expert', 'tensor')
- grad_down: bfloat16 [64, 768, 4096], P('expert', 'tensor')
Inputs may be any that keep to these rules, and one draw needn't show every extreme that they name: `expert_ids`: each row names 8 different experts. Among the 48 tokens of one index of the expert axis no expert is named more than 8 times, and in every draw some expert is named exactly 8 times there.
All inputs are finite; a program needn't handle non-finite values.
Results may differ from a plain program's by a relative error of at most 0.019.
Values may be sent and summed in bfloat16 or wider, within the bound.
No kernel may reach another device: no remote copies, remote signals or barrier semaphores. Data moves between devices by JAX's collectives and lax.ppermute only.
A program may use at most 64 MiB of HBM per device.

v0:
```python
import jax
import jax.numpy as jnp
from jax import lax
from jax.sharding import PartitionSpec as P

TOP = 8


def expert_backward(rows_x, rows_d, w_gate, w_up, w_down):
    gate_pre = jnp.einsum("secd,ehd->sech", rows_x, w_gate, preferred_element_type=jnp.float32)
    up_pre = jnp.einsum("secd,ehd->sech", rows_x, w_up, preferred_element_type=jnp.float32)
    sigmoid = jax.nn.sigmoid(gate_pre)
    active = gate_pre * sigmoid
    hidden = (active * up_pre).astype(jnp.bfloat16)
    hidden_grad = jnp.einsum("secd,ehd->sech", rows_d, w_down, preferred_element_type=jnp.float32)
    up_grad = (hidden_grad * active).astype(jnp.bfloat16)
    gate_grad = (hidden_grad * up_pre * sigmoid * (1.0 + gate_pre * (1.0 - sigmoid))).astype(
        jnp.bfloat16
    )
    grad_gate = jnp.einsum(
        "sech,secd->ehd", gate_grad, rows_x, preferred_element_type=jnp.float32
    ).astype(jnp.bfloat16)
    grad_up = jnp.einsum(
        "sech,secd->ehd", up_grad, rows_x, preferred_element_type=jnp.float32
    ).astype(jnp.bfloat16)
    grad_down = jnp.einsum(
        "sech,secd->ehd", hidden, rows_d, preferred_element_type=jnp.float32
    ).astype(jnp.bfloat16)
    partial_value = jnp.einsum(
        "sech,ehd->secd", gate_grad, w_gate, preferred_element_type=jnp.float32
    )
    partial_value = partial_value + jnp.einsum(
        "sech,ehd->secd", up_grad, w_up, preferred_element_type=jnp.float32
    )
    return (partial_value, grad_gate, grad_up, grad_down)


def on_device(tokens, cotangent, expert_ids, gate_values, w_gate, w_up, w_down):
    tok_count = expert_ids.shape[0]
    local_count = w_gate.shape[0]
    groups = lax.axis_size("expert")
    experts = local_count * groups
    capacity = 4 * tok_count * TOP // (3 * experts)
    feat_width = tokens.shape[1]
    flat_ids = expert_ids.reshape(-1)
    onehot = (flat_ids[:, None] == jnp.arange(experts, dtype=jnp.int32)[None, :]).astype(jnp.int32)
    before = jnp.cumsum(onehot, axis=0) - onehot
    slot_pos = jnp.sum(before * onehot, axis=1)
    target = flat_ids * capacity + slot_pos
    matches = (target[None, :] == jnp.arange(experts * capacity, dtype=jnp.int32)[:, None]).reshape(
        experts * capacity, tok_count, TOP
    )
    by_token = jnp.any(matches, axis=2)
    occupied = jnp.any(by_token, axis=1)
    token_iota = jnp.arange(tok_count, dtype=jnp.int32)
    owner = jnp.sum(jnp.where(by_token, token_iota[None, :], 0), axis=1)
    slot_weight = jnp.sum(jnp.sum(jnp.where(matches, gate_values[None, :, :], 0.0), axis=2), axis=1)
    full_x, full_d = (
        lax.all_gather(tokens, "tensor", axis=1, tiled=True),
        lax.all_gather(cotangent, "tensor", axis=1, tiled=True),
    )
    sent_x = jnp.where(occupied[:, None], full_x[owner], jnp.zeros((), jnp.bfloat16))
    sent_d = (slot_weight[:, None] * full_d[owner].astype(jnp.float32)).astype(jnp.bfloat16)
    buffer_shape = (groups, local_count, capacity, full_x.shape[1])
    sent_x, sent_d = (sent_x.reshape(buffer_shape), sent_d.reshape(buffer_shape))
    rows_x, rows_d = (
        lax.all_to_all(sent_x, "expert", split_axis=0, concat_axis=0, tiled=True),
        lax.all_to_all(sent_d, "expert", split_axis=0, concat_axis=0, tiled=True),
    )
    partial_value, grad_gate, grad_up, grad_down = expert_backward(
        rows_x, rows_d, w_gate, w_up, w_down
    )
    summed = lax.psum(partial_value.astype(jnp.bfloat16), "tensor").astype(jnp.float32)
    returned = lax.dynamic_slice_in_dim(
        summed, lax.axis_index("tensor") * feat_width, feat_width, 3
    ).astype(jnp.bfloat16)
    arrived = lax.all_to_all(returned, "expert", split_axis=0, concat_axis=0, tiled=True).reshape(
        experts * capacity, feat_width
    )
    masked = jnp.where(occupied[:, None], arrived.astype(jnp.float32), jnp.zeros((), jnp.float32))
    grad_tokens = jax.ops.segment_sum(masked, owner, num_segments=tok_count).astype(jnp.bfloat16)
    return (grad_tokens, grad_gate, grad_up, grad_down)


def solution(mesh):
    return jax.shard_map(
        on_device,
        mesh=mesh,
        in_specs=(
            P("expert", "tensor"),
            P("expert", "tensor"),
            P("expert", None),
            P("expert", None),
            P("expert", "tensor", None),
            P("expert", "tensor", None),
            P("expert", "tensor", None),
        ),
        out_specs=(
            P("expert", "tensor"),
            P("expert", "tensor", None),
            P("expert", "tensor", None),
            P("expert", "tensor", None),
        ),
        check_vma=False,
    )
```

profile of v0, /device:TPU:15, one launch (start us, length us, event | category | flops | bytes accessed | tf_op | source)
XLA Modules:
  0.0 448.9 jit_solution(7881900945583448381)
XLA Ops:
  8.2 0.9 reduce-window.6
  11.0 13.7 %all_gather.7 = bf16[48,4096]{1,0:T(8,128)(2,1)S(1)} all-gather(bf16[48,512]{1,0:T(8,128)(2,1)} %param.7), channel_id=1, replica_groups=mesh['expert'=64,'tensor'=8] {'tensor'}, dimensions={1}, use_global_device_ids=true | all-gather | bytes 442368 | tf_op jit(solution)/shard_map/all_gather | solution.py:59
  24.6 4.3 gather_fusion.1
  29.0 4.5 %bitcast_select_fusion = bf16[64,1,8,4096]{3,2,1,0:T(8,128)(2,1)} fusion(bf16[512,4096]{1,0:T(8,128)(2,1)} %gather_fusion.1, pred[64,8]{1,0:T(8,128)(4,1)S(1)} %broadcast_in_dim.73), kind=kLoop, calls=%fused_computation.16 | loop fusion | flops 2097152 | bytes 8389120 | tf_op jit(solution)/shard_map/jit(_where)/select_n | solution.py:62
  33.5 16.3 %all-to-all-start.1 = ((bf16[64,1,8,4096]{3,2,1,0:T(8,128)(2,1)}), bf16[64,1,8,4096]{3,2,1,0:T(8,128)(2,1)}, u32[]{:S(2)}, u32[]{:S(2)}) async-start(bf16[64,1,8,4096]{3,2,1,0:T(8,128)(2,1)} %bitcast_select_fusion), calls=%async_computation.1 | async-start | bytes 8388608 | tf_op jit(solution)/shard_map/all_to_all | solution.py:67
  50.2 13.5 %all_gather.6 = bf16[48,4096]{1,0:T(8,128)(2,1)S(1)} all-gather(bf16[48,512]{1,0:T(8,128)(2,1)S(1)} %copy-done.2), channel_id=1, replica_groups=mesh['expert'=64,'tensor'=8] {'tensor'}, dimensions={1}, use_global_device_ids=true | all-gather | bytes 442368 | tf_op jit(solution)/shard_map/all_gather | solution.py:60
  63.8 4.4 gather_fusion
  68.1 5.6 %fusion = bf16[64,1,8,4096]{3,2,1,0:T(8,128)(2,1)} fusion(bf16[512,4096]{1,0:T(8,128)(2,1)} %gather_fusion, f32[64,8]{1,0:T(8,128)S(1)} %mul.57), kind=kLoop, calls=%fused_computation.4 | loop fusion | flops 6291456 | bytes 8390656 | tf_op jit(solution)/shard_map/convert_element_type | solution.py:63
  73.8 84.2 %all-to-all-done.1 = bf16[64,1,8,4096]{3,2,1,0:T(8,128)(2,1)} async-done(((bf16[64,1,8,4096]{3,2,1,0:T(8,128)(2,1)}), bf16[64,1,8,4096]{3,2,1,0:T(8,128)(2,1)}, u32[]{:S(2)}, u32[]{:S(2)}) %all-to-all-start.1) | async-done | bytes 4194336 | tf_op jit(solution)/shard_map/all_to_all | solution.py:67
  158.0 33.7 %all-to-all-start = ((bf16[64,1,8,4096]{3,2,1,0:T(8,128)(2,1)}), bf16[64,1,8,4096]{3,2,1,0:T(8,128)(2,1)}, u32[]{:S(2)}, u32[]{:S(2)}) async-start(bf16[64,1,8,4096]{3,2,1,0:T(8,128)(2,1)} %fusion), calls=%async_computation | async-start | bytes 8388608 | tf_op jit(solution)/shard_map/all_to_all | solution.py:68
  191.9 3.6 fusion.23
  195.5 3.4 fusion.20
  198.9 105.7 %all-to-all-done = bf16[64,1,8,4096]{3,2,1,0:T(8,128)(2,1)} async-done(((bf16[64,1,8,4096]{3,2,1,0:T(8,128)(2,1)}), bf16[64,1,8,4096]{3,2,1,0:T(8,128)(2,1)}, u32[]{:S(2)}, u32[]{:S(2)}) %all-to-all-start) | async-done | bytes 4194336 | tf_op jit(solution)/shard_map/all_to_all | solution.py:68
  304.6 3.4 fusion.40
  308.1 1.2 fusion.27
  309.3 3.2 fusion.1
  312.6 91.5 %all-reduce.2.cloned.1.call-done = bf16[64,1,8,4096]{3,2,0,1:T(8,128)(2,1)} async-done(((bf16[64,1,8,4096]{3,2,0,1:T(8,128)(2,1)}), bf16[64,1,8,4096]{3,2,0,1:T(8,128)(2,1)}) %all-reduce.2.cloned.1.call-update) | async-done | bytes 4194320 | tf_op jit(solution)/shard_map/psum | solution.py:73
  404.0 1.9 fusion.35
  405.9 12.8 %all-to-all-start.2 = ((bf16[64,1,8,512]{3,2,1,0:T(8,128)(2,1)}), bf16[64,1,8,512]{3,2,1,0:T(8,128)(2,1)S(1)}, u32[]{:S(2)}, u32[]{:S(2)}) async-start(bf16[64,1,8,512]{3,2,1,0:T(8,128)(2,1)} %fusion.35), calls=%async_computation.2 | async-start | bytes 1048576 | tf_op jit(solution)/shard_map/all_to_all | solution.py:77
  418.8 3.9 fusion.6
  422.7 3.9 fusion.7
  426.6 3.9 fusion.5
  430.6 7.1 %all-to-all-done.2 = bf16[64,1,8,512]{3,2,1,0:T(8,128)(2,1)S(1)} async-done(((bf16[64,1,8,512]{3,2,1,0:T(8,128)(2,1)}), bf16[64,1,8,512]{3,2,1,0:T(8,128)(2,1)S(1)}, u32[]{:S(2)}, u32[]{:S(2)}) %all-to-all-start.2) | async-done | bytes 524320 | tf_op jit(solution)/shard_map/all_to_all | solution.py:77
  437.7 3.8 scatter_custom_fusion
  (32 shorter events, 4.1 us)
Async XLA Ops:
  7.2 184.7 %copy-start = (bf16[1,96,4096]{2,1,0:T(8,128)(2,1)S(1)}, bf16[1,96,4096]{2,1,0:T(8,128)(2,1)}, u32[]{:S(2)}) copy-start(bf16[1,96,4096]{2,1,0:T(8,128)(2,1)} %param.11) | copy-start | bytes 2359300
  33.5 16.4 %copy-start.3 = (f32[48,8]{0,1:T(8,128)S(1)}, f32[48,8]{0,1:T(8,128)}, u32[]{:S(2)}) copy-start(f32[48,8]{0,1:T(8,128)} %param.10) | copy-start | bytes 4612
  33.5 16.7 %copy-start.2 = (bf16[48,512]{1,0:T(8,128)(2,1)S(1)}, bf16[48,512]{1,0:T(8,128)(2,1)}, u32[]{:S(2)}) copy-start(bf16[48,512]{1,0:T(8,128)(2,1)} %param.8) | copy-start | bytes 147460
  33.5 124.5 %all-to-all-start.1 = ((bf16[64,1,8,4096]{3,2,1,0:T(8,128)(2,1)}), bf16[64,1,8,4096]{3,2,1,0:T(8,128)(2,1)}, u32[]{:S(2)}, u32[]{:S(2)}) async-start(bf16[64,1,8,4096]{3,2,1,0:T(8,128)(2,1)} %bitcast_select_fusion), calls=%async_computation.1 | async-start | bytes 8388608 | tf_op jit(solution)/shard_map/all_to_all | solution.py:67
  158.0 146.7 %all-to-all-start = ((bf16[64,1,8,4096]{3,2,1,0:T(8,128)(2,1)}), bf16[64,1,8,4096]{3,2,1,0:T(8,128)(2,1)}, u32[]{:S(2)}, u32[]{:S(2)}) async-start(bf16[64,1,8,4096]{3,2,1,0:T(8,128)(2,1)} %fusion), calls=%async_computation | async-start | bytes 8388608 | tf_op jit(solution)/shard_map/all_to_all | solution.py:68
  191.7 3.8 copy-start.1
  191.7 113.0 %copy-start.4 = (bf16[1,96,4096]{2,1,0:T(8,128)(2,1)S(1)}, bf16[1,96,4096]{2,1,0:T(8,128)(2,1)}, u32[]{:S(2)}) copy-start(bf16[1,96,4096]{2,1,0:T(8,128)(2,1)} %param.13) | copy-start | bytes 2359300
  191.7 212.4 %all-reduce.2.cloned.1.call-start = ((), (), s32[]{:S(2)}) async-start(), calls=%async_computation.3 | async-start | bytes 8388608 | tf_op jit(solution)/shard_map/psum | solution.py:73
  405.9 31.7 %all-to-all-start.2 = ((bf16[64,1,8,512]{3,2,1,0:T(8,128)(2,1)}), bf16[64,1,8,512]{3,2,1,0:T(8,128)(2,1)S(1)}, u32[]{:S(2)}, u32[]{:S(2)}) async-start(bf16[64,1,8,512]{3,2,1,0:T(8,128)(2,1)} %fusion.35), calls=%async_computation.2 | async-start | bytes 1048576 | tf_op jit(solution)/shard_map/all_to_all | solution.py:77
Sparse Core Ops, SparseCore 0:
  312.7 91.2 all-reduce.1
where the time goes:
time: 450 us; the launch traced here: 449 us
  waiting for transfers between devices  288 us (64%)
  starting transfers between devices  63.1 us (14%)
  blocking collectives  27.2 us (6%)
  matrix products  26.7 us (6%)
  other arithmetic  18.7 us (4%)
  between operations  14.2 us (3%)
  local copies, waits for them, and re-layouts  10.5 us (2%)
    all_to_all x1, waiting for transfers between devices, on_device(): lax.all_to_all(sent_d, 'expert', split_axis=0, concat_axis=0, tiled=True)  106 us
    psum x1, waiting for transfers between devices, on_device(): lax.psum(partial_value.astype(jnp.bfloat16), 'tensor').astype(jnp.float32)  91.5 us
    all_to_all x1, waiting for transfers between devices, on_device(): lax.all_to_all(sent_x, 'expert', split_axis=0, concat_axis=0, tiled=True)  84.2 us
    all_to_all x1, starting transfers between devices, on_device(): lax.all_to_all(sent_d, 'expert', split_axis=0, concat_axis=0, tiled=True)  33.7 us
    all_to_all x1, starting transfers between devices, on_device(): lax.all_to_all(sent_x, 'expert', split_axis=0, concat_axis=0, tiled=True)  16.3 us
    all_gather x1, blocking collectives, on_device(): lax.all_gather(tokens, 'tensor', axis=1, tiled=True)  13.7 us
    all_gather x1, blocking collectives, on_device(): lax.all_gather(cotangent, 'tensor', axis=1, tiled=True)  13.5 us
    all_to_all x1, starting transfers between devices, on_device(): lax.all_to_all(returned, 'expert', split_axis=0, concat_axis=0, tiled=True)  12.8 us
  transfers between devices with their start and end apart: 4, of which 4 were waited for; matrix products, arithmetic and copies ran while one was open for 6% of the time, Pallas kernels for 0%

commit v1 on v0

--- a/solution.py
+++ b/solution.py
@@ -56,7 +56,9 @@
     owner = jnp.sum(jnp.where(by_token, token_iota[None, :], 0), axis=1)
     slot_weight = jnp.sum(jnp.sum(jnp.where(matches, gate_values[None, :, :], 0.0), axis=2), axis=1)
     full_x, full_d = (
-        lax.all_gather(tokens, "tensor", axis=1, tiled=True),
+        jnp.concatenate(
+            lax.all_to_all(jnp.stack([tokens] * lax.axis_size("tensor")), "tensor", 0, 0), axis=1
+        ),
         lax.all_gather(cotangent, "tensor", axis=1, tiled=True),
     )
     sent_x = jnp.where(occupied[:, None], full_x[owner], jnp.zeros((), jnp.bfloat16))

time: 450 us -> 447 us (level)
  blocking collectives: 27.2 us -> 14.2 us
  waiting for transfers between devices: 288 us -> 299 us
    psum x1, waiting for transfers between devices: 91.5 us -> 107 us  [on_device(): lax.psum(partial_value.astype(jnp.bfloat16), 'tensor').astype(jnp.float32)]
    all_gather x1 -> x0, blocking collectives: 13.7 us -> none  [on_device(): lax.all_gather(tokens, 'tensor', axis=1, tiled=True)]
    all_to_all x1, waiting for transfers between devices: 106 us -> 99 us  [on_device(): lax.all_to_all(sent_d, 'expert', split_axis=0, concat_axis=0, tiled=True)]
    all_to_all x1, starting transfers between devices: 33.7 us -> 27.5 us  [on_device(): lax.all_to_all(sent_d, 'expert', split_axis=0, concat_axis=0, tiled=True)]
    all_to_all x0 -> x1, starting transfers between devices: none -> 5.09 us  [on_device(): lax.all_to_all(jnp.stack([tokens] * lax.axis_size('tensor')), 'tensor', 0...]
  transfers between devices with their start and end apart: 4 -> 5, of which waited for: 4 -> 5; matrix products, arithmetic and copies ran while one was open for 6% -> 7% of each run, Pallas kernels for 0% -> 0%
where the time goes in v1:
time: 447 us; the launch traced here: 446 us
  waiting for transfers between devices  299 us (67%)
  starting transfers between devices  62 us (14%)
  matrix products  26.7 us (6%)
  other arithmetic  18.7 us (4%)
  blocking collectives  14.2 us (3%)
  between operations  14.2 us (3%)
  local copies, waits for them, and re-layouts  12.1 us (3%)
    psum x1, waiting for transfers between devices, on_device(): lax.psum(partial_value.astype(jnp.bfloat16), 'tensor').astype(jnp.float32)  107 us
    all_to_all x1, waiting for transfers between devices, on_device(): lax.all_to_all(sent_d, 'expert', split_axis=0, concat_axis=0, tiled=True)  99 us
    all_to_all x1, waiting for transfers between devices, on_device(): lax.all_to_all(sent_x, 'expert', split_axis=0, concat_axis=0, tiled=True)  83.2 us
    all_to_all x1, starting transfers between devices, on_device(): lax.all_to_all(sent_d, 'expert', split_axis=0, concat_axis=0, tiled=True)  27.5 us
    all_to_all x1, starting transfers between devices, on_device(): lax.all_to_all(sent_x, 'expert', split_axis=0, concat_axis=0, tiled=True)  16.3 us
    all_gather x1, blocking collectives, on_device(): lax.all_gather(cotangent, 'tensor', axis=1, tiled=True)  14.2 us
    all_to_all x1, starting transfers between devices, on_device(): lax.all_to_all(returned, 'expert', split_axis=0, concat_axis=0, tiled=True)  12.8 us
  transfers between devices with their start and end apart: 5, of which 5 were waited for; matrix products, arithmetic and copies ran while one was open for 7% of the time, Pallas kernels for 0%

profile of v1, /device:TPU:15, one launch (start us, length us, event | category | flops | bytes accessed | tf_op | source)
XLA Modules:
  0.0 446.5 jit_solution(2468524915834146209)
XLA Ops:
  7.2 1.6 stack.2
  8.8 5.1 %all-to-all-start.1 = ((bf16[8,48,512]{2,1,0:T(8,128)(2,1)}), bf16[8,48,512]{2,1,0:T(8,128)(2,1)S(1)}, u32[]{:S(2)}, u32[]{:S(2)}) async-start(bf16[8,48,512]{2,1,0:T(8,128)(2,1)} %stack.2), calls=%async_computation.1 | async-start | bytes 786432 | tf_op jit(solution)/shard_map/all_to_all | solution.py:60
  17.6 2.7 all-to-all-done.1
  20.3 4.4 gather_fusion.1
  24.7 4.5 %bitcast_select_fusion = bf16[64,1,8,4096]{3,2,1,0:T(8,128)(2,1)} fusion(bf16[512,4096]{1,0:T(8,128)(2,1)} %gather_fusion.1, pred[64,8]{1,0:T(8,128)(4,1)S(1)} %broadcast_in_dim.73), kind=kLoop, calls=%fused_computation.16 | loop fusion | flops 2097152 | bytes 8389120 | tf_op jit(solution)/shard_map/jit(_where)/select_n | solution.py:64
  29.2 16.3 %all-to-all-start.2 = ((bf16[64,1,8,4096]{3,2,1,0:T(8,128)(2,1)}), bf16[64,1,8,4096]{3,2,1,0:T(8,128)(2,1)}, u32[]{:S(2)}, u32[]{:S(2)}) async-start(bf16[64,1,8,4096]{3,2,1,0:T(8,128)(2,1)} %bitcast_select_fusion), calls=%async_computation.2 | async-start | bytes 8388608 | tf_op jit(solution)/shard_map/all_to_all | solution.py:69
  45.9 14.2 %all_gather.3 = bf16[48,4096]{1,0:T(8,128)(2,1)S(1)} all-gather(bf16[48,512]{1,0:T(8,128)(2,1)S(1)} %copy-done.2), channel_id=1, replica_groups=mesh['expert'=64,'tensor'=8] {'tensor'}, dimensions={1}, use_global_device_ids=true | all-gather | bytes 442368 | tf_op jit(solution)/shard_map/all_gather | solution.py:62
  60.1 4.4 gather_fusion
  64.5 5.6 %fusion = bf16[64,1,8,4096]{3,2,1,0:T(8,128)(2,1)} fusion(bf16[512,4096]{1,0:T(8,128)(2,1)} %gather_fusion, f32[64,8]{1,0:T(8,128)S(1)} %mul.57), kind=kLoop, calls=%fused_computation.4 | loop fusion | flops 6291456 | bytes 8390656 | tf_op jit(solution)/shard_map/convert_element_type | solution.py:65
  70.1 83.2 %all-to-all-done.2 = bf16[64,1,8,4096]{3,2,1,0:T(8,128)(2,1)} async-done(((bf16[64,1,8,4096]{3,2,1,0:T(8,128)(2,1)}), bf16[64,1,8,4096]{3,2,1,0:T(8,128)(2,1)}, u32[]{:S(2)}, u32[]{:S(2)}) %all-to-all-start.2) | async-done | bytes 4194336 | tf_op jit(solution)/shard_map/all_to_all | solution.py:69
  153.3 27.5 %all-to-all-start = ((bf16[64,1,8,4096]{3,2,1,0:T(8,128)(2,1)}), bf16[64,1,8,4096]{3,2,1,0:T(8,128)(2,1)}, u32[]{:S(2)}, u32[]{:S(2)}) async-start(bf16[64,1,8,4096]{3,2,1,0:T(8,128)(2,1)} %fusion), calls=%async_computation | async-start | bytes 8388608 | tf_op jit(solution)/shard_map/all_to_all | solution.py:70
  181.1 3.6 fusion.23
  184.7 3.4 fusion.20
  188.1 99.0 %all-to-all-done = bf16[64,1,8,4096]{3,2,1,0:T(8,128)(2,1)} async-done(((bf16[64,1,8,4096]{3,2,1,0:T(8,128)(2,1)}), bf16[64,1,8,4096]{3,2,1,0:T(8,128)(2,1)}, u32[]{:S(2)}, u32[]{:S(2)}) %all-to-all-start) | async-done | bytes 4194336 | tf_op jit(solution)/shard_map/all_to_all | solution.py:70
  287.1 3.4 fusion.40
  291.8 3.2 fusion.1
  295.0 106.6 %all-reduce.2.cloned.1.call-done = bf16[64,1,8,4096]{3,2,0,1:T(8,128)(2,1)} async-done(((bf16[64,1,8,4096]{3,2,0,1:T(8,128)(2,1)}), bf16[64,1,8,4096]{3,2,0,1:T(8,128)(2,1)}) %all-reduce.2.cloned.1.call-update) | async-done | bytes 4194320 | tf_op jit(solution)/shard_map/psum | solution.py:75
  401.6 1.9 fusion.35
  403.5 12.8 %all-to-all-start.3 = ((bf16[64,1,8,512]{3,2,1,0:T(8,128)(2,1)}), bf16[64,1,8,512]{3,2,1,0:T(8,128)(2,1)S(1)}, u32[]{:S(2)}, u32[]{:S(2)}) async-start(bf16[64,1,8,512]{3,2,1,0:T(8,128)(2,1)} %fusion.35), calls=%async_computation.3 | async-start | bytes 1048576 | tf_op jit(solution)/shard_map/all_to_all | solution.py:79
  416.4 3.9 fusion.6
  420.3 3.9 fusion.7
  424.2 3.9 fusion.5
  428.2 7.1 %all-to-all-done.3 = bf16[64,1,8,512]{3,2,1,0:T(8,128)(2,1)S(1)} async-done(((bf16[64,1,8,512]{3,2,1,0:T(8,128)(2,1)}), bf16[64,1,8,512]{3,2,1,0:T(8,128)(2,1)S(1)}, u32[]{:S(2)}, u32[]{:S(2)}) %all-to-all-start.3) | async-done | bytes 524320 | tf_op jit(solution)/shard_map/all_to_all | solution.py:79
  435.3 3.8 scatter_custom_fusion
  (35 shorter events, 6.1 us)
Async XLA Ops:
  7.2 173.9 %copy-start = (bf16[1,96,4096]{2,1,0:T(8,128)(2,1)S(1)}, bf16[1,96,4096]{2,1,0:T(8,128)(2,1)}, u32[]{:S(2)}) copy-start(bf16[1,96,4096]{2,1,0:T(8,128)(2,1)} %param.11) | copy-start | bytes 2359300
  8.8 11.5 %all-to-all-start.1 = ((bf16[8,48,512]{2,1,0:T(8,128)(2,1)}), bf16[8,48,512]{2,1,0:T(8,128)(2,1)S(1)}, u32[]{:S(2)}, u32[]{:S(2)}) async-start(bf16[8,48,512]{2,1,0:T(8,128)(2,1)} %stack.2), calls=%async_computation.1 | async-start | bytes 786432 | tf_op jit(solution)/shard_map/all_to_all | solution.py:60
  29.2 16.4 %copy-start.3 = (f32[48,8]{0,1:T(8,128)S(1)}, f32[48,8]{0,1:T(8,128)}, u32[]{:S(2)}) copy-start(f32[48,8]{0,1:T(8,128)} %param.10) | copy-start | bytes 4612
  29.2 16.7 %copy-start.2 = (bf16[48,512]{1,0:T(8,128)(2,1)S(1)}, bf16[48,512]{1,0:T(8,128)(2,1)}, u32[]{:S(2)}) copy-start(bf16[48,512]{1,0:T(8,128)(2,1)} %param.8) | copy-start | bytes 147460
  29.2 124.1 %all-to-all-start.2 = ((bf16[64,1,8,4096]{3,2,1,0:T(8,128)(2,1)}), bf16[64,1,8,4096]{3,2,1,0:T(8,128)(2,1)}, u32[]{:S(2)}, u32[]{:S(2)}) async-start(bf16[64,1,8,4096]{3,2,1,0:T(8,128)(2,1)} %bitcast_select_fusion), calls=%async_computation.2 | async-start | bytes 8388608 | tf_op jit(solution)/shard_map/all_to_all | solution.py:69
  153.3 133.8 %all-to-all-start = ((bf16[64,1,8,4096]{3,2,1,0:T(8,128)(2,1)}), bf16[64,1,8,4096]{3,2,1,0:T(8,128)(2,1)}, u32[]{:S(2)}, u32[]{:S(2)}) async-start(bf16[64,1,8,4096]{3,2,1,0:T(8,128)(2,1)} %fusion), calls=%async_computation | async-start | bytes 8388608 | tf_op jit(solution)/shard_map/all_to_all | solution.py:70
  180.8 3.8 copy-start.1
  180.8 106.3 %copy-start.4 = (bf16[1,96,4096]{2,1,0:T(8,128)(2,1)S(1)}, bf16[1,96,4096]{2,1,0:T(8,128)(2,1)}, u32[]{:S(2)}) copy-start(bf16[1,96,4096]{2,1,0:T(8,128)(2,1)} %param.13) | copy-start | bytes 2359300
  180.8 220.8 %all-reduce.2.cloned.1.call-start = ((), (), s32[]{:S(2)}) async-start(), calls=%async_computation.4 | async-start | bytes 8388608 | tf_op jit(solution)/shard_map/psum | solution.py:75
  403.5 31.7 %all-to-all-start.3 = ((bf16[64,1,8,512]{3,2,1,0:T(8,128)(2,1)}), bf16[64,1,8,512]{3,2,1,0:T(8,128)(2,1)S(1)}, u32[]{:S(2)}, u32[]{:S(2)}) async-start(bf16[64,1,8,512]{3,2,1,0:T(8,128)(2,1)} %fusion.35), calls=%async_computation.3 | async-start | bytes 1048576 | tf_op jit(solution)/shard_map/all_to_all | solution.py:79
Sparse Core Ops, SparseCore 0:
  295.1 106.4 all-reduce.1
